TPU v7x, 512 devices: a whole 4x8x8 slice. The times are simulated.
512 devices in a mesh: expert: 128 (over y, z, core), dp: 4 (over x).
Axes of the slice: x: 4, y: 8, z: 8, core: 2. Of those that a mesh axis runs over, the one named last changes fastest.
Arguments:
- hidden: bfloat16 [128, 4, 256, 1024], P('expert', 'dp'), may hold values from -6 to 6
- w_down: bfloat16 [128, 1024, 3584], P('expert', 'dp'), may hold values from -0.1875 to 0.1875
- expert_ids: int32 [4, 2048, 8], P('dp', 'expert'), may hold values from 0 to 127, all different within a row; in each aligned block of 16 rows (0 to 15, 16 to 31, ..., all dimensions but the last counted through in order) at most 2 rows name the same one
- route_weights: float32 [4, 2048, 8], P('dp', 'expert'), may hold values from 0.1 to 0.6
- grad_out: bfloat16 [4, 2048, 3584], P('dp', 'expert'), may hold values from -6 to 6
Outputs:
- mixed: bfloat16 [4, 2048, 3584], P('dp', 'expert')
- d_hidden: bfloat16 [128, 4, 256, 1024], P('expert', 'dp')
- d_w_down: bfloat16 [128, 1024, 3584], P('expert', 'dp')
- d_route: float32 [4, 2048, 8], P('dp', 'expert')
Inputs may be any that keep to these rules, and one draw needn't show every extreme that they name: `expert_ids`: among the 16 tokens of one device no expert is chosen more than 2 times, and some expert is chosen exactly 2 times; the 8 choices of a token are distinct.
All inputs are finite; a program needn't handle non-finite values.
Results may differ from a plain program's by a relative error of at most 0.0085.
Values may be sent and summed in bfloat16 or wider, within the bound.
A program may use at most 128 MiB of HBM per device.

v0:
```python
import jax
import jax.numpy as jnp
from jax import lax
from jax.sharding import PartitionSpec as P


def slot_ranks(choices, experts):
    flat = choices.reshape(-1)
    onehot = (flat[:, None] == jnp.arange(experts, dtype=jnp.int32)[None, :]).astype(jnp.int32)
    earlier = jnp.cumsum(onehot, axis=0) - onehot
    return jnp.sum(earlier * onehot, axis=1).reshape(choices.shape)


def on_device(hidden, w_down, expert_ids, route_weights, grad_out):
    experts = lax.axis_size("expert")
    groups = lax.axis_size("dp")
    slots = hidden.shape[2] // experts
    width = w_down.shape[2]
    w_whole = lax.all_gather(w_down, "dp", axis=1, tiled=True)[0]
    out_slots = jnp.dot(hidden[0, 0], w_whole, preferred_element_type=jnp.float32).astype(
        jnp.bfloat16
    )
    arrived = lax.all_to_all(
        out_slots.reshape(experts, slots, width), "expert", split_axis=0, concat_axis=0, tiled=True
    )
    arrived = arrived.reshape(experts * slots, width)
    choices = expert_ids[0]
    weights = route_weights[0]
    cotangent = grad_out[0].astype(jnp.float32)
    rows = choices * slots + slot_ranks(choices, experts)
    out_pair = arrived[rows].astype(jnp.float32)
    mixed = jnp.einsum("tk,tkd->td", weights, out_pair)
    d_route = jnp.einsum("td,tkd->tk", cotangent, out_pair)
    grad_pair = (weights[..., None] * cotangent[:, None, :]).astype(jnp.bfloat16)
    outgoing = jnp.zeros((experts * slots, width), jnp.bfloat16)
    outgoing = outgoing.at[rows.reshape(-1)].set(grad_pair.reshape(-1, width))
    mine = lax.all_to_all(
        outgoing.reshape(experts, 1, slots, width),
        "expert",
        split_axis=0,
        concat_axis=0,
        tiled=True,
    )
    own_grads = mine[:, 0]
    d_hidden = jnp.einsum(
        "rd,hd->rh", own_grads.reshape(-1, width), w_whole, preferred_element_type=jnp.float32
    ).astype(jnp.bfloat16)
    columns = lax.all_to_all(hidden, "dp", split_axis=3, concat_axis=1, tiled=True)[0]
    columns = columns.reshape(groups, experts, slots, columns.shape[-1])
    cw = width // 2
    parts = []
    for c in range(2):
        slot_grads = lax.all_gather(mine[..., c * cw : (c + 1) * cw], "dp", axis=1, tiled=True)
        parts.append(
            jnp.einsum(
                "gsch,sgcd->hd", columns, slot_grads, preferred_element_type=jnp.float32
            ).astype(jnp.bfloat16)
        )
    d_weight = jnp.concatenate(parts, axis=1)
    return (
        mixed.astype(jnp.bfloat16)[None],
        d_hidden.reshape(hidden.shape),
        d_weight[None],
        d_route[None],
    )


def solution(mesh):
    placed = (
        P("expert", "dp", None, None),
        P("expert", "dp", None),
        P("dp", "expert", None),
        P("dp", "expert", None),
        P("dp", "expert", None),
    )
    return jax.shard_map(
        on_device,
        mesh=mesh,
        in_specs=placed,
        out_specs=(
            P("dp", "expert", None),
            P("expert", "dp", None, None),
            P("expert", "dp", None),
            P("dp", "expert", None),
        ),
        check_vma=False,
    )
```

profile of v0, /device:TPU:1, one launch (start us, length us, event | category | flops | bytes accessed | tf_op | source)
XLA Modules:
  0.0 227.6 jit_solution(7683013739206800182)
XLA Ops:
  7.2 0.7 all-gather.4.cloned.1.call-update
  8.6 0.2 reduce_window_sum.11
  8.8 0.2 select_reduce_fusion
  9.0 2.5 %scatter_custom_fusion = bf16[256,3584]{1,0:T(8,128)(2,1)S(1)} fusion(s32[128]{0:T(128)S(1)} %fusion.33, f32[16,3584]{1,0:T(8,128)S(1)} %bitcast_convert_fusion.1, f32[128]{0:T(128)S(1)} %mul.53, bf16[]{:T(256)} %constant.7.clone.1), kind=kCustom, calls=%fused_computation.18 | custom fusion | flops 917504 | bytes 2064898 | tf_op jit(solution)/shard_map/scatter | solution.py:36
  11.5 1.6 reshape.99
  13.2 64.9 %all_to_all.25 = bf16[128,1,2,3584]{3,2,1,0:T(2,128)(2,1)S(1)} all-to-all(bf16[128,1,2,3584]{3,2,1,0:T(2,128)(2,1)} %bitcast.87), channel_id=1, replica_groups=mesh['expert'=128,'dp'=4] {'expert'}, dimensions={0} | all-to-all | bytes 3670016 | tf_op jit(solution)/shard_map/all_to_all | solution.py:37
  78.1 2.2 fusion.34
  80.2 3.6 %copy.71 = bf16[128,1,2,1792]{0,3,1,2:T(8,128)(2,1)} copy(bf16[128,1,2,1792]{3,2,1,0:T(2,128)(2,1)} %get-tuple-element.24) | data formatting | bytes 1835008
  83.9 2.1 copy.72
  86.0 0.9 copy.58
  86.9 0.5 broadcast.58
  87.4 3.8 %reduce = bf16[1024,256]{1,0:T(8,128)(2,1)S(1)} reduce(bf16[1024,1,1,256]{3,2,1,0:T(2,128)(2,1)S(1)} %bitcast.89, bf16[]{:T(256)} %broadcast.58), dimensions={1,2}, to_apply=%bitcast.78.reduce_sub_computation | reduce | bytes 1048578
  91.3 0.9 reshape.126
  92.2 4.0 %all-to-all-start.2 = ((bf16[4,2,32768]{2,1,0:T(2,128)(2,1)}), bf16[4,2,32768]{2,1,0:T(2,128)(2,1)S(1)}, u32[]{:S(2)}, u32[]{:S(2)}) async-start(bf16[4,2,32768]{2,1,0:T(2,128)(2,1)} %reshape.126), calls=%async_computation.2 | async-start | bytes 1048576 | tf_op jit(solution)/shard_map/all_to_all | solution.py:48
  96.2 6.4 %fusion.4 = bf16[256,3584]{1,0:T(8,128)(2,1)} fusion(bf16[1,1024,3584]{2,1,0:T(8,128)(2,1)} %all-gather.4.cloned.1.call-done, bf16[1,1,256,1024]{3,2,1,0:T(8,128)(2,1)S(1)} %copy-done.1), kind=kOutput, calls=%fused_computation.6 | convolution fusion | flops 1879965696 | bytes 9699328 | tf_op jit(solution)/shard_map/dot_general | solution.py:20
  102.6 4.8 %reshape.96 = bf16[128,2,3584]{2,1,0:T(2,128)(2,1)} reshape(bf16[256,3584]{1,0:T(8,128)(2,1)} %fusion.4) | data formatting | bytes 3670016 | tf_op jit(solution)/shard_map/reshape | solution.py:24
  107.3 15.9 %all-to-all-start = ((bf16[128,2,3584]{2,1,0:T(2,128)(2,1)}), bf16[128,2,3584]{2,1,0:T(2,128)(2,1)}, u32[]{:S(2)}, u32[]{:S(2)}) async-start(bf16[128,2,3584]{2,1,0:T(2,128)(2,1)} %reshape.96), calls=%async_computation | async-start | bytes 3670016 | tf_op jit(solution)/shard_map/all_to_all | solution.py:23
  123.6 0.5 reshape.127
  124.3 1.1 copy.59
  125.3 1.7 reshape_squeeze.6
  127.0 22.5 %all-gather.6.cloned.1.call-done = bf16[128,4,2,1792]{0,3,1,2:T(8,128)(2,1)} async-done(((bf16[128,1,2,1792]{0,3,1,2:T(8,128)(2,1)}), bf16[128,4,2,1792]{0,3,1,2:T(8,128)(2,1)}) %all-gather.6.cloned.1.call-update) | async-done | bytes 3670032 | tf_op jit(solution)/shard_map/all_gather | solution.py:53
  149.5 3.2 %fusion.10 = bf16[256,1792]{0,1:T(8,128)(2,1)S(1)} fusion(bf16[128,4,2,1792]{0,3,1,2:T(8,128)(2,1)} %all-gather.6.cloned.1.call-done, bf16[4,128,2,256]{3,0,2,1:T(4,128)(2,1)S(1)} %bitcast.91), kind=kOutput, calls=%fused_computation.12 | convolution fusion | flops 939982848 | bytes 5111808 | tf_op jit(solution)/shard_map/gsch,sgcd->hd/dot_general | solution.py:55
  152.7 48.4 %all-gather.8.cloned.1.call-done = bf16[128,4,2,1792]{0,3,1,2:T(8,128)(2,1)} async-done(((bf16[128,1,2,1792]{0,3,1,2:T(8,128)(2,1)}), bf16[128,4,2,1792]{0,3,1,2:T(8,128)(2,1)}) %all-gather.8.cloned.1.call-update) | async-done | bytes 3670032 | tf_op jit(solution)/shard_map/all_gather | solution.py:53
  201.1 3.2 %fusion.9 = bf16[256,1792]{0,1:T(8,128)(2,1)S(1)} fusion(bf16[128,4,2,1792]{0,3,1,2:T(8,128)(2,1)} %all-gather.8.cloned.1.call-done, bf16[4,128,2,256]{3,0,2,1:T(4,128)(2,1)S(1)} %bitcast.92), kind=kOutput, calls=%fused_computation.11 | convolution fusion | flops 939982848 | bytes 5111808 | tf_op jit(solution)/shard_map/gsch,sgcd->hd/dot_general | solution.py:55
  204.4 2.6 %copy.63 = bf16[1,256,3584]{2,1,0:T(8,128)(2,1)} copy(bf16[1,256,3584]{1,2,0:T(8,128)(2,1)S(1)} %maximum_bitcast_fusion) | data formatting | bytes 3670016
  207.0 6.5 %fusion.15 = bf16[1,1,256,1024]{3,2,1,0:T(8,128)(2,1)} fusion(bf16[256,3584]{1,0:T(8,128)(2,1)} %reshape_squeeze.6, bf16[1,1024,3584]{2,1,0:T(8,128)(2,1)} %all-gather.4.cloned.1.call-done), kind=kOutput, calls=%fused_computation.17 | convolution fusion | flops 1879310336 | bytes 9699328 | tf_op jit(solution)/shard_map/rd,hd->rh/dot_general | solution.py:45
  213.5 4.1 %reshape.97 = bf16[256,3584]{1,0:T(8,128)(2,1)S(1)} reshape(bf16[128,2,3584]{2,1,0:T(2,128)(2,1)} %all-to-all-done) | data formatting | bytes 3670016 | tf_op jit(solution)/shard_map/reshape | solution.py:26
  217.6 1.1 gather_fusion
  218.7 0.6 fusion.22
  219.3 0.4 fusion.20
  219.7 0.7 copy.82
  220.4 0.7 copy.69
  (39 shorter events, 1.4 us)
Async XLA Ops:
  7.2 0.8 copy-start.4
  7.2 1.1 copy-start.5
  7.2 1.8 copy-start.3
  7.2 89.0 %all-gather.4.cloned.1.call-start = ((), (), s32[]{:S(2)}) async-start(), calls=%async_computation.3 | async-start | bytes 9175040 | tf_op jit(solution)/shard_map/all_gather | solution.py:19
  7.9 141.6 %all-gather.6.cloned.1.call-start = ((), (), s32[]{:S(2)}) async-start(), calls=%async_computation.4 | async-start | bytes 4587520 | tf_op jit(solution)/shard_map/all_gather | solution.py:53
  83.8 2.2 copy-start
  83.8 117.3 %all-gather.8.cloned.1.call-start = ((), (), s32[]{:S(2)}) async-start(), calls=%async_computation.5 | async-start | bytes 4587520 | tf_op jit(solution)/shard_map/all_gather | solution.py:53
  91.3 4.9 %copy-start.1 = (bf16[1,1,256,1024]{3,2,1,0:T(8,128)(2,1)S(1)}, bf16[1,1,256,1024]{3,2,1,0:T(8,128)(2,1)}, u32[]{:S(2)}) copy-start(bf16[1,1,256,1024]{3,2,1,0:T(8,128)(2,1)} %param.5) | copy-start | bytes 1572868
  92.2 15.2 %all-to-all-start.2 = ((bf16[4,2,32768]{2,1,0:T(2,128)(2,1)}), bf16[4,2,32768]{2,1,0:T(2,128)(2,1)S(1)}, u32[]{:S(2)}, u32[]{:S(2)}) async-start(bf16[4,2,32768]{2,1,0:T(2,128)(2,1)} %reshape.126), calls=%async_computation.2 | async-start | bytes 1048576 | tf_op jit(solution)/shard_map/all_to_all | solution.py:48
  107.3 106.2 %all-to-all-start = ((bf16[128,2,3584]{2,1,0:T(2,128)(2,1)}), bf16[128,2,3584]{2,1,0:T(2,128)(2,1)}, u32[]{:S(2)}, u32[]{:S(2)}) async-start(bf16[128,2,3584]{2,1,0:T(2,128)(2,1)} %reshape.96), calls=%async_computation | async-start | bytes 3670016 | tf_op jit(solution)/shard_map/all_to_all | solution.py:23
  125.3 24.2 %copy-start.2 = (bf16[1,4,1,256,256]{4,1,3,2,0:T(4,128)(2,1)S(1)}, bf16[1,4,1,256,256]{4,1,3,2,0:T(4,128)(2,1)}, u32[]{:S(2)}) copy-start(bf16[1,4,1,256,256]{4,1,3,2,0:T(4,128)(2,1)} %copy.59) | copy-start | bytes 1572868
Sparse Core Ops, SparseCore 0:
  10.1 84.9 all-gather.3
  97.2 52.2 all-gather.5
  151.6 49.4 all-gather.7
where the time goes:
time: 228 us
  waiting for transfers between devices  71.7 us (31%)
  blocking collectives  64.9 us (28%)
  local copies, waits for them, and re-layouts  29.9 us (13%)
  matrix products  20.3 us (9%)
  starting transfers between devices  20 us (9%)
  between operations  14 us (6%)
  other arithmetic  6.95 us (3%)
    all_gather x2, waiting for transfers between devices, on_device(): lax.all_gather(mine[..., c * cw:(c + 1) * cw], 'dp', axis=1, tiled=True)  70.9 us
    all_to_all x1, blocking collectives, on_device(): lax.all_to_all(outgoing.reshape(experts, 1, slots, width), 'expert', spli...  64.9 us
    all_to_all x1, starting transfers between devices, on_device(): lax.all_to_all(out_slots.reshape(experts, slots, width), 'expert', split_...  15.9 us
    unnamed x22, local copies, waits for them, and re-layouts  11.3 us
    dot_general x1, matrix products, on_device(): jnp.einsum('rd,hd->rh', own_grads.reshape(-1, width), w_whole, preferred_...  6.53 us
    dot_general x1, matrix products, on_device(): jnp.dot(hidden[0, 0], w_whole, preferred_element_type=jnp.float32)  6.37 us
    dot_general x2, matrix products, on_device(): jnp.einsum('gsch,sgcd->hd', columns, slot_grads, preferred_element_type=j...  6.36 us
    reshape x1, local copies, waits for them, and re-layouts, on_device(): out_slots.reshape(experts, slots, width)  4.77 us
  transfers between devices with their start and end apart: 5, of which 2 were waited for; matrix products, arithmetic and copies ran while one was open for 22% of the time, Pallas kernels for 0%

commit v1 on v0

--- a/solution.py
+++ b/solution.py
@@ -2,6 +2,27 @@
 import jax.numpy as jnp
 from jax import lax
 from jax.sharding import PartitionSpec as P
+
+
+def gather_around(array, axis, dim):
+    length, mine, rows = (lax.axis_size(axis), lax.axis_index(axis), array.shape[dim])
+    ahead = [(i, (i + 1) % length) for i in range(length)]
+    downward = [(i, (i - 1) % length) for i in range(length)]
+    whole = jnp.zeros((*array.shape[:dim], length * rows, *array.shape[dim + 1 :]), array.dtype)
+    whole = lax.dynamic_update_slice_in_dim(whole, array, mine * rows, axis=dim)
+    from_left = from_right = array
+    halfway = length // 2
+    for step in range(1, halfway + 1):
+        from_left = lax.ppermute(from_left, axis, ahead)
+        whole = lax.dynamic_update_slice_in_dim(
+            whole, from_left, (mine - step) % length * rows, axis=dim
+        )
+        if step < length - halfway:
+            from_right = lax.ppermute(from_right, axis, downward)
+            whole = lax.dynamic_update_slice_in_dim(
+                whole, from_right, (mine + step) % length * rows, axis=dim
+            )
+    return whole
 
 
 def slot_ranks(choices, experts):
@@ -50,7 +71,7 @@
     cw = width // 2
     parts = []
     for c in range(2):
-        slot_grads = lax.all_gather(mine[..., c * cw : (c + 1) * cw], "dp", axis=1, tiled=True)
+        slot_grads = gather_around(mine[..., c * cw : (c + 1) * cw], "dp", 1)
         parts.append(
             jnp.einsum(
                 "gsch,sgcd->hd", columns, slot_grads, preferred_element_type=jnp.float32

time: 228 us -> 220 us (0.965)
  blocking collectives: 64.9 us -> 0 us
  starting transfers between devices: 20 us -> 52.1 us
  local copies, waits for them, and re-layouts: 29.9 us -> 58 us
  matrix products: 20.3 us -> 17.3 us
    all_gather x2 -> x0, waiting for transfers between devices: 70.9 us -> none  [on_device(): lax.all_gather(mine[..., c * cw:(c + 1) * cw], 'dp', axis=1, tiled=True)]
    all_to_all x1 -> x0, blocking collectives: 64.9 us -> none  [on_device(): lax.all_to_all(outgoing.reshape(experts, 1, slots, width), 'expert', spli...]
    all_to_all x0 -> x1, waiting for transfers between devices: none -> 44.3 us  [on_device(): lax.all_to_all(outgoing.reshape(experts, 1, slots, width), 'expert', spli...]
    ppermute x0 -> x6, waiting for transfers between devices: none -> 23.4 us  [the longest x4 23.4 us: gather_around(): from_left = lax.ppermute(from_left, axis, ahead)]
    all_to_all x0 -> x1, starting transfers between devices: none -> 20.4 us  [on_device(): lax.all_to_all(outgoing.reshape(experts, 1, slots, width), 'expert', spli...]
    ppermute x0 -> x6, local copies, waits for them, and re-layouts: none -> 17.7 us  [the longest x4 10.4 us: gather_around(): from_left = lax.ppermute(from_left, axis, ahead)]
    ppermute x0 -> x6, starting transfers between devices: none -> 17.4 us  [the longest x2 9.06 us: gather_around(): from_right = lax.ppermute(from_right, axis, downward)]
    dynamic_update_slice x0 -> x8, local copies, waits for them, and re-layouts: none -> 7.22 us  [the longest x4 4.04 us: gather_around(): lax.dynamic_update_slice_in_dim(whole, from_left, (mine - step) % length...]
  transfers between devices with their start and end apart: 5 -> 10, of which waited for: 2 -> 4; matrix products, arithmetic and copies ran while one was open for 22% -> 33% of each run, Pallas kernels for 0% -> 0%
where the time goes in v1:
time: 220 us; the launch traced here: 219 us
  waiting for transfers between devices  70.2 us (32%)
  local copies, waits for them, and re-layouts  58 us (26%)
  starting transfers between devices  52.1 us (24%)
  matrix products  17.3 us (8%)
  between operations  14.4 us (7%)
  other arithmetic  6.96 us (3%)
    all_to_all x1, waiting for transfers between devices, on_device(): lax.all_to_all(outgoing.reshape(experts, 1, slots, width), 'expert', spli...  44.3 us
    ppermute x4, waiting for transfers between devices, gather_around(): from_left = lax.ppermute(from_left, axis, ahead)  23.4 us
    all_to_all x1, starting transfers between devices, on_device(): lax.all_to_all(outgoing.reshape(experts, 1, slots, width), 'expert', spli...  20.4 us
    ppermute x4, local copies, waits for them, and re-layouts, gather_around(): from_left = lax.ppermute(from_left, axis, ahead)  10.4 us
    all_to_all x1, starting transfers between devices, on_device(): lax.all_to_all(out_slots.reshape(experts, slots, width), 'expert', split_...  9.45 us
    unnamed x28, local copies, waits for them, and re-layouts  9.09 us
    ppermute x2, starting transfers between devices, gather_around(): from_right = lax.ppermute(from_right, axis, downward)  9.06 us
    ppermute x4, starting transfers between devices, gather_around(): from_left = lax.ppermute(from_left, axis, ahead)  8.3 us
  transfers between devices with their start and end apart: 10, of which 4 were waited for; matrix products, arithmetic and copies ran while one was open for 33% of the time, Pallas kernels for 0%

profile of v1, /device:TPU:1, one launch (start us, length us, event | category | flops | bytes accessed | tf_op | source)
XLA Modules:
  0.0 219.0 jit_solution(12615234433244323887)
XLA Ops:
  7.9 2.4 %copy.60 = bf16[1,1,256,1024]{2,1,0,3:T(2,128)(2,1)S(1)} copy(bf16[1,1,256,1024]{3,2,1,0:T(8,128)(2,1)} %param.5) | data formatting | bytes 1048576 | tf_op args[0]
  10.9 3.8 %reduce = bf16[1024,256]{1,0:T(8,128)(2,1)S(1)} reduce(bf16[1024,1,1,256]{3,2,1,0:T(2,128)(2,1)S(1)} %bitcast.88, bf16[]{:T(256)} %broadcast.65), dimensions={1,2}, to_apply=%bitcast.78.reduce_sub_computation | reduce | bytes 1048578
  15.6 4.8 %all-to-all-start.2 = ((bf16[4,2,32768]{2,1,0:T(2,128)(2,1)}), bf16[4,2,32768]{2,1,0:T(2,128)(2,1)S(1)}, u32[]{:S(2)}, u32[]{:S(2)}) async-start(bf16[4,2,32768]{2,1,0:T(2,128)(2,1)} %reshape.126), calls=%async_computation.2 | async-start | bytes 1048576 | tf_op jit(solution)/shard_map/all_to_all | solution.py:69
  21.4 2.5 %scatter_custom_fusion = bf16[256,3584]{1,0:T(8,128)(2,1)S(1)} fusion(s32[128]{0:T(128)S(1)} %fusion.33, f32[16,3584]{1,0:T(8,128)S(1)} %bitcast_convert_fusion.1, f32[128]{0:T(128)S(1)} %mul.53, bf16[]{:T(256)} %constant.46.clone.1), kind=kCustom, calls=%fused_computation.18 | custom fusion | flops 917504 | bytes 2064898 | tf_op jit(solution)/shard_map/scatter | solution.py:57
  25.6 1.7 all-to-all-done.2
  27.4 20.4 %all-to-all-start.1 = ((bf16[128,1,2,3584]{3,2,1,0:T(2,128)(2,1)}), bf16[128,1,2,3584]{3,2,1,0:T(2,128)(2,1)S(1)}, u32[]{:S(2)}, u32[]{:S(2)}) async-start(bf16[128,1,2,3584]{3,2,1,0:T(2,128)(2,1)} %bitcast.86), calls=%async_computation.1 | async-start | bytes 3670016 | tf_op jit(solution)/shard_map/all_to_all | solution.py:58
  49.9 44.3 %all-to-all-done.1 = bf16[128,1,2,3584]{3,2,1,0:T(2,128)(2,1)S(1)} async-done(((bf16[128,1,2,3584]{3,2,1,0:T(2,128)(2,1)}), bf16[128,1,2,3584]{3,2,1,0:T(2,128)(2,1)S(1)}, u32[]{:S(2)}, u32[]{:S(2)}) %all-to-all-start.1) | async-done | bytes 1835040 | tf_op jit(solution)/shard_map/all_to_all | solution.py:58
  94.3 2.2 fusion.34
  96.4 3.6 %copy.63 = bf16[128,1,2,1792]{0,3,1,2:T(8,128)(2,1)} copy(bf16[128,1,2,1792]{3,2,1,0:T(2,128)(2,1)} %get-tuple-element.21) | data formatting | bytes 1835008 | tf_op jit(solution)/shard_map/slice | solution.py:74
  100.0 2.3 %collective-permute-start.3 = (bf16[128,1,2,1792]{3,2,1,0:T(2,128)(2,1)}, bf16[128,1,2,1792]{3,2,1,0:T(2,128)(2,1)}, u32[]{:S(2)}, u32[]{:S(2)}) collective-permute-start(bf16[128,1,2,1792]{3,2,1,0:T(2,128)(2,1)} %get-tuple-element.21), channel_id=1, source_target_pairs={{0,1},{1,2},{2,3},{3,0},{4,5},{5,6},{6,7},{7,4},{8,9},{9,10},{10,1... | collective-permute-start | bytes 2752520 | tf_op jit(solution)/shard_map/ppermute | solution.py:16
  102.4 4.3 %collective-permute-start.4 = (bf16[128,1,2,1792]{3,2,1,0:T(2,128)(2,1)}, bf16[128,1,2,1792]{3,2,1,0:T(2,128)(2,1)}, u32[]{:S(2)}, u32[]{:S(2)}) collective-permute-start(bf16[128,1,2,1792]{3,2,1,0:T(2,128)(2,1)} %get-tuple-element.21), channel_id=1, source_target_pairs={{0,3},{1,0},{2,1},{3,2},{4,7},{5,4},{6,5},{7,6},{8,11},{9,8},{10,9... | collective-permute-start | bytes 2752520 | tf_op jit(solution)/shard_map/ppermute | solution.py:21
  106.7 1.9 collective-permute-start
  108.6 4.8 %collective-permute-start.1 = (bf16[128,1,2,1792]{3,2,1,0:T(2,128)(2,1)S(1)}, bf16[128,1,2,1792]{3,2,1,0:T(2,128)(2,1)}, u32[]{:S(2)}, u32[]{:S(2)}) collective-permute-start(bf16[128,1,2,1792]{3,2,1,0:T(2,128)(2,1)S(1)} %get-tuple-element.20), channel_id=1, source_target_pairs={{0,3},{1,0},{2,1},{3,2},{4,7},{5,4},{6,5},{7,6},{8,11},{9,8},{10,9... | collective-permute-start | bytes 2752520 | tf_op jit(solution)/shard_map/ppermute | solution.py:21
  113.4 2.4 %broadcast.59.clone = bf16[128,4,2,1792]{0,3,1,2:T(8,128)(2,1)} broadcast(bf16[]{:T(256)} %constant.46.clone.1), dimensions={} | broadcast | bytes 3670018 | tf_op jit(solution)/shard_map/broadcast.1
  116.8 2.1 copy.56
  120.5 5.3 %fusion.4 = bf16[256,3584]{1,0:T(8,128)(2,1)S(1)} fusion(bf16[1,1024,3584]{2,1,0:T(8,128)(2,1)} %all-gather.2.cloned.1.call-done, bf16[1,1,256,1024]{3,2,1,0:T(8,128)(2,1)} %param.5), kind=kOutput, calls=%fused_computation.6 | convolution fusion | flops 1879965696 | bytes 9699328 | tf_op jit(solution)/shard_map/dot_general | solution.py:41
  127.6 9.4 %all-to-all-start = ((bf16[128,2,3584]{2,1,0:T(2,128)(2,1)}), bf16[128,2,3584]{2,1,0:T(2,128)(2,1)}, u32[]{:S(2)}, u32[]{:S(2)}) async-start(bf16[128,2,3584]{2,1,0:T(2,128)(2,1)} %reshape.96), calls=%async_computation | async-start | bytes 3670016 | tf_op jit(solution)/shard_map/all_to_all | solution.py:44
  137.6 1.9 copy-done.4
  139.5 2.6 %copy.64 = bf16[128,1,2,1792]{0,3,1,2:T(8,128)(2,1)S(1)} copy(bf16[128,1,2,1792]{3,2,1,0:T(2,128)(2,1)} %collective-permute-done.3) | data formatting | bytes 1835008 | tf_op jit(solution)/shard_map/ppermute | solution.py:16
  142.2 1.9 collective-permute-start.5
  144.1 2.6 %copy.57 = bf16[128,1,2,1792]{0,3,1,2:T(8,128)(2,1)S(1)} copy(bf16[128,1,2,1792]{3,2,1,0:T(2,128)(2,1)} %collective-permute-done) | data formatting | bytes 1835008 | tf_op jit(solution)/shard_map/ppermute | solution.py:16
  146.7 2.1 collective-permute-start.2
  148.9 3.6 %copy.65 = bf16[128,1,2,1792]{0,3,1,2:T(8,128)(2,1)} copy(bf16[128,1,2,1792]{3,2,1,0:T(2,128)(2,1)} %collective-permute-done.4) | data formatting | bytes 1835008 | tf_op jit(solution)/shard_map/ppermute | solution.py:21
  152.5 3.7 %copy.58 = bf16[128,1,2,1792]{0,3,1,2:T(8,128)(2,1)} copy(bf16[128,1,2,1792]{3,2,1,0:T(2,128)(2,1)} %collective-permute-done.1) | data formatting | bytes 1835008 | tf_op jit(solution)/shard_map/ppermute | solution.py:21
  160.2 6.3 %collective-permute-done.5 = bf16[128,1,2,1792]{3,2,1,0:T(2,128)(2,1)} collective-permute-done((bf16[128,1,2,1792]{3,2,1,0:T(2,128)(2,1)}, bf16[128,1,2,1792]{3,2,1,0:T(2,128)(2,1)}, u32[]{:S(2)}, u32[]{:S(2)}) %collective-permute-start.5) | collective-permute-done | bytes 917536 | tf_op jit(solution)/shard_map/ppermute | solution.py:16
  166.5 2.6 %copy.66 = bf16[128,1,2,1792]{0,3,1,2:T(8,128)(2,1)S(1)} copy(bf16[128,1,2,1792]{3,2,1,0:T(2,128)(2,1)} %collective-permute-done.5) | data formatting | bytes 1835008 | tf_op jit(solution)/shard_map/ppermute | solution.py:16
  169.1 17.0 %collective-permute-done.2 = bf16[128,1,2,1792]{3,2,1,0:T(2,128)(2,1)} collective-permute-done((bf16[128,1,2,1792]{3,2,1,0:T(2,128)(2,1)}, bf16[128,1,2,1792]{3,2,1,0:T(2,128)(2,1)}, u32[]{:S(2)}, u32[]{:S(2)}) %collective-permute-start.2) | collective-permute-done | bytes 917536 | tf_op jit(solution)/shard_map/ppermute | solution.py:16
  186.2 2.6 %copy.59 = bf16[128,1,2,1792]{0,3,1,2:T(8,128)(2,1)S(1)} copy(bf16[128,1,2,1792]{3,2,1,0:T(2,128)(2,1)} %collective-permute-done.2) | data formatting | bytes 1835008 | tf_op jit(solution)/shard_map/ppermute | solution.py:16
  190.9 3.3 %fusion.9 = bf16[256,1792]{0,1:T(8,128)(2,1)S(1)} fusion(bf16[128,4,2,1792]{0,3,1,2:T(8,128)(2,1)} %constant_dynamic-update-slice_fusion.7, bf16[4,128,2,256]{3,0,2,1:T(4,128)(2,1)S(1)} %bitcast.90), kind=kOutput, calls=%fused_computation.11 | convolution fusion | flops 939982848 | bytes 5111808 | tf_op jit(solution)/shard_map/gsch,sgcd->hd/dot_general | solution.py:76
  195.5 2.6 %copy.68 = bf16[1,256,3584]{2,1,0:T(8,128)(2,1)} copy(bf16[1,256,3584]{1,2,0:T(8,128)(2,1)S(1)} %maximum_bitcast_fusion) | data formatting | bytes 3670016
  198.1 6.5 %fusion.15 = bf16[1,1,256,1024]{3,2,1,0:T(8,128)(2,1)} fusion(bf16[256,3584]{1,0:T(8,128)(2,1)} %reshape_squeeze.6, bf16[1,1024,3584]{2,1,0:T(8,128)(2,1)} %all-gather.2.cloned.1.call-done), kind=kOutput, calls=%fused_computation.17 | convolution fusion | flops 1879310336 | bytes 9699328 | tf_op jit(solution)/shard_map/rd,hd->rh/dot_general | solution.py:66
  204.6 4.1 %reshape.97 = bf16[256,3584]{1,0:T(8,128)(2,1)S(1)} reshape(bf16[128,2,3584]{2,1,0:T(2,128)(2,1)} %all-to-all-done) | data formatting | bytes 3670016 | tf_op jit(solution)/shard_map/reshape | solution.py:47
  (70 shorter events, 22.6 us)
Async XLA Ops:
  7.2 13.3 %copy-start.8 = (s32[1,16,8]{1,2,0:T(8,128)S(1)}, s32[1,16,8]{1,2,0:T(8,128)}, u32[]{:S(2)}) copy-start(s32[1,16,8]{1,2,0:T(8,128)} %param.7) | copy-start | bytes 1540
  7.2 13.5 %copy-start.7 = (bf16[1,16,3584]{2,1,0:T(8,128)(2,1)S(1)}, bf16[1,16,3584]{2,1,0:T(8,128)(2,1)}, u32[]{:S(2)}) copy-start(bf16[1,16,3584]{2,1,0:T(8,128)(2,1)} %param.9) | copy-start | bytes 344068
  7.2 13.7 %copy-start.9 = (f32[1,16,8]{1,2,0:T(8,128)S(1)}, f32[1,16,8]{1,2,0:T(8,128)}, u32[]{:S(2)}) copy-start(f32[1,16,8]{1,2,0:T(8,128)} %param.8) | copy-start | bytes 1540
  7.2 113.3 %all-gather.2.cloned.1.call-start = ((), (), s32[]{:S(2)}) async-start(), calls=%async_computation.3 | async-start | bytes 9175040 | tf_op jit(solution)/shard_map/all_gather | solution.py:40
  15.6 11.8 %all-to-all-start.2 = ((bf16[4,2,32768]{2,1,0:T(2,128)(2,1)}), bf16[4,2,32768]{2,1,0:T(2,128)(2,1)S(1)}, u32[]{:S(2)}, u32[]{:S(2)}) async-start(bf16[4,2,32768]{2,1,0:T(2,128)(2,1)} %reshape.126), calls=%async_computation.2 | async-start | bytes 1048576 | tf_op jit(solution)/shard_map/all_to_all | solution.py:69
  27.4 66.9 %all-to-all-start.1 = ((bf16[128,1,2,3584]{3,2,1,0:T(2,128)(2,1)}), bf16[128,1,2,3584]{3,2,1,0:T(2,128)(2,1)S(1)}, u32[]{:S(2)}, u32[]{:S(2)}) async-start(bf16[128,1,2,3584]{3,2,1,0:T(2,128)(2,1)} %bitcast.86), calls=%async_computation.1 | async-start | bytes 3670016 | tf_op jit(solution)/shard_map/all_to_all | solution.py:58
  100.0 15.7 %copy-start = (bf16[128,1,2,1792]{0,3,1,2:T(8,128)(2,1)S(1)}, bf16[128,1,2,1792]{0,3,1,2:T(8,128)(2,1)}, u32[]{:S(2)}) copy-start(bf16[128,1,2,1792]{0,3,1,2:T(8,128)(2,1)} %copy.63) | copy-start | bytes 2752516
  100.0 39.5 %collective-permute-start.3 = (bf16[128,1,2,1792]{3,2,1,0:T(2,128)(2,1)}, bf16[128,1,2,1792]{3,2,1,0:T(2,128)(2,1)}, u32[]{:S(2)}, u32[]{:S(2)}) collective-permute-start(bf16[128,1,2,1792]{3,2,1,0:T(2,128)(2,1)} %get-tuple-element.21), channel_id=1, source_target_pairs={{0,1},{1,2},{2,3},{3,0},{4,5},{5,6},{6,7},{7,4},{8,9},{9,10},{10,1... | collective-permute-start | bytes 2752520 | tf_op jit(solution)/shard_map/ppermute | solution.py:16
  102.4 46.5 %collective-permute-start.4 = (bf16[128,1,2,1792]{3,2,1,0:T(2,128)(2,1)}, bf16[128,1,2,1792]{3,2,1,0:T(2,128)(2,1)}, u32[]{:S(2)}, u32[]{:S(2)}) collective-permute-start(bf16[128,1,2,1792]{3,2,1,0:T(2,128)(2,1)} %get-tuple-element.21), channel_id=1, source_target_pairs={{0,3},{1,0},{2,1},{3,2},{4,7},{5,4},{6,5},{7,6},{8,11},{9,8},{10,9... | collective-permute-start | bytes 2752520 | tf_op jit(solution)/shard_map/ppermute | solution.py:21
  106.7 37.4 %collective-permute-start = (bf16[128,1,2,1792]{3,2,1,0:T(2,128)(2,1)S(1)}, bf16[128,1,2,1792]{3,2,1,0:T(2,128)(2,1)}, u32[]{:S(2)}, u32[]{:S(2)}) collective-permute-start(bf16[128,1,2,1792]{3,2,1,0:T(2,128)(2,1)S(1)} %get-tuple-element.20), channel_id=1, source_target_pairs={{0,1},{1,2},{2,3},{3,0},{4,5},{5,6},{6,7},{7,4},{8,9},{9,10},{10,1... | collective-permute-start | bytes 2752520 | tf_op jit(solution)/shard_map/ppermute | solution.py:16
  108.6 43.9 %collective-permute-start.1 = (bf16[128,1,2,1792]{3,2,1,0:T(2,128)(2,1)S(1)}, bf16[128,1,2,1792]{3,2,1,0:T(2,128)(2,1)}, u32[]{:S(2)}, u32[]{:S(2)}) collective-permute-start(bf16[128,1,2,1792]{3,2,1,0:T(2,128)(2,1)S(1)} %get-tuple-element.20), channel_id=1, source_target_pairs={{0,3},{1,0},{2,1},{3,2},{4,7},{5,4},{6,5},{7,6},{8,11},{9,8},{10,9... | collective-permute-start | bytes 2752520 | tf_op jit(solution)/shard_map/ppermute | solution.py:21
  127.6 9.9 %copy-start.1 = (bf16[128,1,2,1792]{0,3,1,2:T(8,128)(2,1)S(1)}, bf16[128,1,2,1792]{0,3,1,2:T(8,128)(2,1)}, u32[]{:S(2)}) copy-start(bf16[128,1,2,1792]{0,3,1,2:T(8,128)(2,1)} %copy.56) | copy-start | bytes 2752516
  127.6 77.0 %all-to-all-start = ((bf16[128,2,3584]{2,1,0:T(2,128)(2,1)}), bf16[128,2,3584]{2,1,0:T(2,128)(2,1)}, u32[]{:S(2)}, u32[]{:S(2)}) async-start(bf16[128,2,3584]{2,1,0:T(2,128)(2,1)} %reshape.96), calls=%async_computation | async-start | bytes 3670016 | tf_op jit(solution)/shard_map/all_to_all | solution.py:44
  137.6 1.9 copy-start.4
  142.2 24.4 %collective-permute-start.5 = (bf16[128,1,2,1792]{3,2,1,0:T(2,128)(2,1)}, bf16[128,1,2,1792]{3,2,1,0:T(2,128)(2,1)}, u32[]{:S(2)}, u32[]{:S(2)}) collective-permute-start(bf16[128,1,2,1792]{3,2,1,0:T(2,128)(2,1)} %collective-permute-done.3), channel_id=1, source_target_pairs={{0,1},{1,2},{2,3},{3,0},{4,5},{5,6},{6,7},{7,4},{8,9},{9,10},{10,1... | collective-permute-start | bytes 2752520 | tf_op jit(solution)/shard_map/ppermute | solution.py:16
  146.7 39.5 %collective-permute-start.2 = (bf16[128,1,2,1792]{3,2,1,0:T(2,128)(2,1)}, bf16[128,1,2,1792]{3,2,1,0:T(2,128)(2,1)}, u32[]{:S(2)}, u32[]{:S(2)}) collective-permute-start(bf16[128,1,2,1792]{3,2,1,0:T(2,128)(2,1)} %collective-permute-done), channel_id=1, source_target_pairs={{0,1},{1,2},{2,3},{3,0},{4,5},{5,6},{6,7},{7,4},{8,9},{9,10},{10,1... | collective-permute-start | bytes 2752520 | tf_op jit(solution)/shard_map/ppermute | solution.py:16
  152.5 5.7 %copy-start.2 = (bf16[128,1,2,1792]{0,3,1,2:T(8,128)(2,1)S(1)}, bf16[128,1,2,1792]{0,3,1,2:T(8,128)(2,1)}, u32[]{:S(2)}) copy-start(bf16[128,1,2,1792]{0,3,1,2:T(8,128)(2,1)} %copy.65) | copy-start | bytes 2752516
  156.1 3.0 %copy-start.3 = (bf16[128,1,2,1792]{0,3,1,2:T(8,128)(2,1)S(1)}, bf16[128,1,2,1792]{0,3,1,2:T(8,128)(2,1)}, u32[]{:S(2)}) copy-start(bf16[128,1,2,1792]{0,3,1,2:T(8,128)(2,1)} %copy.58) | copy-start | bytes 2752516
  160.2 30.7 %copy-start.6 = (bf16[1,4,1,256,256]{4,1,3,2,0:T(4,128)(2,1)S(1)}, bf16[1,4,1,256,256]{4,1,3,2,0:T(4,128)(2,1)}, u32[]{:S(2)}) copy-start(bf16[1,4,1,256,256]{4,1,3,2,0:T(4,128)(2,1)} %copy.61) | copy-start | bytes 1572868
  190.8 3.3 %copy-start.5 = (bf16[128,4,2,1792]{0,3,1,2:T(8,128)(2,1)S(1)}, bf16[128,4,2,1792]{0,3,1,2:T(8,128)(2,1)}, u32[]{:S(2)}) copy-start(bf16[128,4,2,1792]{0,3,1,2:T(8,128)(2,1)} %constant_dynamic-update-slice_fusion.3) | copy-start | bytes 11010052
Sparse Core Ops, SparseCore 0:
  10.1 84.9 all-gather.1
